TPU v7x, 256 devices: a whole 4x4x8 slice. The times are simulated.
256 devices in a mesh: layer: 8 (over y, core), feat: 32 (over z, x).
Axes of the slice: x: 4, y: 4, z: 8, core: 2. Of those that a mesh axis runs over, the one named last changes fastest.
Arguments:
- top_grad: bfloat16 [256, 4608], P('feat'), may hold values from -6 to 6
- decoder: bfloat16 [8, 16384, 4608], P('layer', 'feat'), may hold values from -0.09375 to 0.09375
- encoder: bfloat16 [8, 16384, 4608], P('layer', 'feat'), may hold values from -0.03125 to 0.03125
- activations: bfloat16 [8, 256, 16384], P('layer', None, 'feat'), may hold values from 0.099609375 to 3
- block_ids: int32 [8, 32, 64], P('layer'), may hold values from 0 to 127, all different within a row
- block_counts: int32 [8, 32], P('layer'), may hold values from 1 to 64, 1024 in all within a row
Outputs:
- attribution: bfloat16 [8, 256, 16384], P('layer', None, 'feat')
- grads: float32 [8, 256, 4608], P('layer', 'feat')
Inputs may be any that keep to these rules, and one draw needn't show every extreme that they name: `block_ids`: within one row of the last dimension the ids are distinct; every block id appears somewhere. `block_counts`: for each layer the counts sum to 1024, and some tile of each layer has exactly 64.
All inputs are finite; a program needn't handle non-finite values.
Results may differ from a plain program's by a relative error of at most 0.024.
Values may be sent and summed in bfloat16 or wider, within the bound.
A program may use at most 64 MiB of HBM per device.

v0:
```python
import jax
import jax.numpy as jnp
from jax import lax
from jax.sharding import PartitionSpec as P

BLOCK = 128


def passed_along(value, axis, steps):
    count = lax.axis_size(axis)
    first, last = (max(0, -steps), min(count, count - steps))
    return lax.ppermute(value, axis, [(source, source + steps) for source in range(first, last)])


def body(top_grad, decoder, encoder, activations, block_ids, block_counts):
    layer_count = lax.axis_size("layer")
    tile_count = lax.axis_size("feat")
    section_index = lax.axis_index("layer")
    feat_index = lax.axis_index("feat")
    dec_rows = decoder[0]
    enc_rows = encoder[0]
    feat_dev = dec_rows.shape[0]
    model_width = dec_rows.shape[1]
    blk_dev = feat_dev // BLOCK
    tok_dev = top_grad.shape[0]
    list_width = block_ids.shape[2]
    listed = jnp.arange(list_width, dtype=jnp.int32)[None, :] < block_counts[0][:, None]
    owned = feat_index * blk_dev + jnp.arange(blk_dev, dtype=jnp.int32)
    matches = (block_ids[0][:, :, None] == owned[None, None, :]) & listed[:, :, None]
    tile_mask = jnp.any(matches, axis=1).astype(jnp.bfloat16)
    gated = (
        activations[0].reshape(tile_count, tok_dev, blk_dev, BLOCK) * tile_mask[:, None, :, None]
    )
    gated = gated.reshape(tile_count, tok_dev, feat_dev)
    group_count = 4
    group_rows = tok_dev // group_count
    step_total = group_count + layer_count - 1
    is_top = section_index == layer_count - 1

    def advance(step_count, carry):
        incoming, attr_buf, grad_buf = carry
        group_index = step_count - (layer_count - 1 - section_index)
        is_live = (group_index >= 0) & (group_index < group_count)
        group_slot = jnp.clip(group_index, 0, group_count - 1)
        row_offset = group_slot * group_rows
        top_rows = lax.dynamic_slice_in_dim(top_grad, row_offset, group_rows, 0).astype(jnp.float32)
        upstream = jnp.where(is_top, top_rows, incoming)
        gate_rows = lax.dynamic_slice_in_dim(gated, row_offset, group_rows, 1).reshape(
            tile_count * group_rows, feat_dev
        )
        scores = lax.dot_general(
            lax.all_gather(upstream.astype(jnp.bfloat16), "feat", axis=0, tiled=True),
            dec_rows,
            (((1,), (1,)), ((), ())),
            preferred_element_type=jnp.float32,
        )
        attributed = (scores * gate_rows).astype(jnp.bfloat16)
        summed = lax.psum_scatter(
            jnp.dot(attributed, enc_rows, preferred_element_type=jnp.float32).astype(jnp.bfloat16),
            "feat",
            scatter_dimension=0,
            tiled=True,
        ).astype(jnp.float32)
        updated = upstream + summed
        old_attr = lax.dynamic_slice_in_dim(attr_buf, row_offset, group_rows, 1)
        new_attr = jnp.where(
            is_live, attributed.reshape(tile_count, group_rows, feat_dev), old_attr
        )
        attr_buf = lax.dynamic_update_slice_in_dim(attr_buf, new_attr, row_offset, 1)
        old_grad = lax.dynamic_slice_in_dim(grad_buf, row_offset, group_rows, 0)
        new_grad = jnp.where(is_live, updated, old_grad)
        grad_buf = lax.dynamic_update_slice_in_dim(grad_buf, new_grad, row_offset, 0)
        passed = passed_along(updated.astype(jnp.bfloat16), "layer", -1).astype(updated.dtype)
        return (passed, attr_buf, grad_buf)

    start_state = (
        jnp.zeros((group_rows, model_width), jnp.float32),
        jnp.zeros((tile_count, tok_dev, feat_dev), jnp.bfloat16),
        jnp.zeros((tok_dev, model_width), jnp.float32),
    )
    final_state = lax.fori_loop(0, step_total, advance, start_state)
    attr_out = final_state[1].reshape(1, tile_count * tok_dev, feat_dev)
    grad_out = final_state[2][None]
    return (attr_out, grad_out)


def solution(mesh):
    placed = (
        P("feat", None),
        P("layer", "feat", None),
        P("layer", "feat", None),
        P("layer", None, "feat"),
        P("layer", None, None),
        P("layer", None),
    )
    return jax.shard_map(
        body,
        mesh=mesh,
        in_specs=placed,
        out_specs=(P("layer", None, "feat"), P("layer", "feat", None)),
        check_vma=False,
    )
```

profile of v0, /device:TPU:1, one launch (start us, length us, event | category | flops | bytes accessed | tf_op | source)
XLA Modules:
  0.0 2294.9 jit_solution(4350635033827040506)
XLA Ops:
  10.1 2277.4 %while.20 = (s32[]{:T(128)}, f32[2,4608]{1,0:T(2,128)S(1)}, bf16[32,8,512]{2,1,0:T(8,128)(2,1)S(1)}, f32[8,4608]{1,0:T(8,128)S(1)}, pred[]{:T(512)}, /*index=5*/...) while((s32[]{:T(128)}, f32[2,4608]{1,0:T(2,128)S(1)}, ...), condition=%wide.region_3.4_spmd.clone, body=%wide.region_1.3_spmd.clone.sunk | while | flops 604802048 | bytes 36239852 | solution.py:81
  11.1 42.2 %all-gather.3 = bf16[32,2,4608]{2,1,0:T(2,128)(2,1)S(1)} all-gather(bf16[1,2,4608]{2,1,0:T(2,128)(2,1)S(1)} %convert_bitcast_fusion.2), channel_id=1, replica_groups=mesh['layer'=8,'feat'=32] {'feat'}, dimensions={0}, use_global_device_ids=true | all-gather | bytes 608256 | tf_op jit(solution)/shard_map/while/body/eval_jaxpr/all_gather | solution.py:52
  60.8 152.3 %all-reduce.5.cloned.1.call-done = bf16[64,4608]{1,0:T(8,128)(2,1)} async-done(((bf16[64,4608]{1,0:T(8,128)(2,1)}), bf16[64,4608]{1,0:T(8,128)(2,1)}) %all-reduce.5.cloned.1.call-update) | async-done | bytes 589840 | tf_op jit(solution)/shard_map/while
  224.8 36.7 %all-gather.3 = bf16[32,2,4608]{2,1,0:T(2,128)(2,1)S(1)} all-gather(bf16[1,2,4608]{2,1,0:T(2,128)(2,1)S(1)} %convert_bitcast_fusion.2), channel_id=1, replica_groups=mesh['layer'=8,'feat'=32] {'feat'}, dimensions={0}, use_global_device_ids=true | all-gather | bytes 608256 | tf_op jit(solution)/shard_map/while/body/eval_jaxpr/all_gather | solution.py:52
  269.0 150.5 %all-reduce.5.cloned.1.call-done = bf16[64,4608]{1,0:T(8,128)(2,1)} async-done(((bf16[64,4608]{1,0:T(8,128)(2,1)}), bf16[64,4608]{1,0:T(8,128)(2,1)}) %all-reduce.5.cloned.1.call-update) | async-done | bytes 589840 | tf_op jit(solution)/shard_map/while
  431.2 36.7 %all-gather.3 = bf16[32,2,4608]{2,1,0:T(2,128)(2,1)S(1)} all-gather(bf16[1,2,4608]{2,1,0:T(2,128)(2,1)S(1)} %convert_bitcast_fusion.2), channel_id=1, replica_groups=mesh['layer'=8,'feat'=32] {'feat'}, dimensions={0}, use_global_device_ids=true | all-gather | bytes 608256 | tf_op jit(solution)/shard_map/while/body/eval_jaxpr/all_gather | solution.py:52
  475.4 150.5 %all-reduce.5.cloned.1.call-done = bf16[64,4608]{1,0:T(8,128)(2,1)} async-done(((bf16[64,4608]{1,0:T(8,128)(2,1)}), bf16[64,4608]{1,0:T(8,128)(2,1)}) %all-reduce.5.cloned.1.call-update) | async-done | bytes 589840 | tf_op jit(solution)/shard_map/while
  637.6 36.7 %all-gather.3 = bf16[32,2,4608]{2,1,0:T(2,128)(2,1)S(1)} all-gather(bf16[1,2,4608]{2,1,0:T(2,128)(2,1)S(1)} %convert_bitcast_fusion.2), channel_id=1, replica_groups=mesh['layer'=8,'feat'=32] {'feat'}, dimensions={0}, use_global_device_ids=true | all-gather | bytes 608256 | tf_op jit(solution)/shard_map/while/body/eval_jaxpr/all_gather | solution.py:52
  681.8 150.5 %all-reduce.5.cloned.1.call-done = bf16[64,4608]{1,0:T(8,128)(2,1)} async-done(((bf16[64,4608]{1,0:T(8,128)(2,1)}), bf16[64,4608]{1,0:T(8,128)(2,1)}) %all-reduce.5.cloned.1.call-update) | async-done | bytes 589840 | tf_op jit(solution)/shard_map/while
  833.2 7.2 collective-permute-start
  843.9 36.7 %all-gather.3 = bf16[32,2,4608]{2,1,0:T(2,128)(2,1)S(1)} all-gather(bf16[1,2,4608]{2,1,0:T(2,128)(2,1)S(1)} %convert_bitcast_fusion.2), channel_id=1, replica_groups=mesh['layer'=8,'feat'=32] {'feat'}, dimensions={0}, use_global_device_ids=true | all-gather | bytes 608256 | tf_op jit(solution)/shard_map/while/body/eval_jaxpr/all_gather | solution.py:52
  888.1 150.5 %all-reduce.5.cloned.1.call-done = bf16[64,4608]{1,0:T(8,128)(2,1)} async-done(((bf16[64,4608]{1,0:T(8,128)(2,1)}), bf16[64,4608]{1,0:T(8,128)(2,1)}) %all-reduce.5.cloned.1.call-update) | async-done | bytes 589840 | tf_op jit(solution)/shard_map/while
  1050.3 36.7 %all-gather.3 = bf16[32,2,4608]{2,1,0:T(2,128)(2,1)S(1)} all-gather(bf16[1,2,4608]{2,1,0:T(2,128)(2,1)S(1)} %convert_bitcast_fusion.2), channel_id=1, replica_groups=mesh['layer'=8,'feat'=32] {'feat'}, dimensions={0}, use_global_device_ids=true | all-gather | bytes 608256 | tf_op jit(solution)/shard_map/while/body/eval_jaxpr/all_gather | solution.py:52
  1094.5 150.5 %all-reduce.5.cloned.1.call-done = bf16[64,4608]{1,0:T(8,128)(2,1)} async-done(((bf16[64,4608]{1,0:T(8,128)(2,1)}), bf16[64,4608]{1,0:T(8,128)(2,1)}) %all-reduce.5.cloned.1.call-update) | async-done | bytes 589840 | tf_op jit(solution)/shard_map/while
  1256.7 36.7 %all-gather.3 = bf16[32,2,4608]{2,1,0:T(2,128)(2,1)S(1)} all-gather(bf16[1,2,4608]{2,1,0:T(2,128)(2,1)S(1)} %convert_bitcast_fusion.2), channel_id=1, replica_groups=mesh['layer'=8,'feat'=32] {'feat'}, dimensions={0}, use_global_device_ids=true | all-gather | bytes 608256 | tf_op jit(solution)/shard_map/while/body/eval_jaxpr/all_gather | solution.py:52
  1300.9 150.5 %all-reduce.5.cloned.1.call-done = bf16[64,4608]{1,0:T(8,128)(2,1)} async-done(((bf16[64,4608]{1,0:T(8,128)(2,1)}), bf16[64,4608]{1,0:T(8,128)(2,1)}) %all-reduce.5.cloned.1.call-update) | async-done | bytes 589840 | tf_op jit(solution)/shard_map/while
  1463.1 36.7 %all-gather.3 = bf16[32,2,4608]{2,1,0:T(2,128)(2,1)S(1)} all-gather(bf16[1,2,4608]{2,1,0:T(2,128)(2,1)S(1)} %convert_bitcast_fusion.2), channel_id=1, replica_groups=mesh['layer'=8,'feat'=32] {'feat'}, dimensions={0}, use_global_device_ids=true | all-gather | bytes 608256 | tf_op jit(solution)/shard_map/while/body/eval_jaxpr/all_gather | solution.py:52
  1507.3 150.5 %all-reduce.5.cloned.1.call-done = bf16[64,4608]{1,0:T(8,128)(2,1)} async-done(((bf16[64,4608]{1,0:T(8,128)(2,1)}), bf16[64,4608]{1,0:T(8,128)(2,1)}) %all-reduce.5.cloned.1.call-update) | async-done | bytes 589840 | tf_op jit(solution)/shard_map/while
  1669.4 36.7 %all-gather.3 = bf16[32,2,4608]{2,1,0:T(2,128)(2,1)S(1)} all-gather(bf16[1,2,4608]{2,1,0:T(2,128)(2,1)S(1)} %convert_bitcast_fusion.2), channel_id=1, replica_groups=mesh['layer'=8,'feat'=32] {'feat'}, dimensions={0}, use_global_device_ids=true | all-gather | bytes 608256 | tf_op jit(solution)/shard_map/while/body/eval_jaxpr/all_gather | solution.py:52
  1713.6 150.5 %all-reduce.5.cloned.1.call-done = bf16[64,4608]{1,0:T(8,128)(2,1)} async-done(((bf16[64,4608]{1,0:T(8,128)(2,1)}), bf16[64,4608]{1,0:T(8,128)(2,1)}) %all-reduce.5.cloned.1.call-update) | async-done | bytes 589840 | tf_op jit(solution)/shard_map/while
  1875.8 36.7 %all-gather.3 = bf16[32,2,4608]{2,1,0:T(2,128)(2,1)S(1)} all-gather(bf16[1,2,4608]{2,1,0:T(2,128)(2,1)S(1)} %convert_bitcast_fusion.2), channel_id=1, replica_groups=mesh['layer'=8,'feat'=32] {'feat'}, dimensions={0}, use_global_device_ids=true | all-gather | bytes 608256 | tf_op jit(solution)/shard_map/while/body/eval_jaxpr/all_gather | solution.py:52
  1920.0 150.5 %all-reduce.5.cloned.1.call-done = bf16[64,4608]{1,0:T(8,128)(2,1)} async-done(((bf16[64,4608]{1,0:T(8,128)(2,1)}), bf16[64,4608]{1,0:T(8,128)(2,1)}) %all-reduce.5.cloned.1.call-update) | async-done | bytes 589840 | tf_op jit(solution)/shard_map/while
  2082.2 36.7 %all-gather.3 = bf16[32,2,4608]{2,1,0:T(2,128)(2,1)S(1)} all-gather(bf16[1,2,4608]{2,1,0:T(2,128)(2,1)S(1)} %convert_bitcast_fusion.2), channel_id=1, replica_groups=mesh['layer'=8,'feat'=32] {'feat'}, dimensions={0}, use_global_device_ids=true | all-gather | bytes 608256 | tf_op jit(solution)/shard_map/while/body/eval_jaxpr/all_gather | solution.py:52
  2126.4 150.5 %all-reduce.5.cloned.1.call-done = bf16[64,4608]{1,0:T(8,128)(2,1)} async-done(((bf16[64,4608]{1,0:T(8,128)(2,1)}), bf16[64,4608]{1,0:T(8,128)(2,1)}) %all-reduce.5.cloned.1.call-update) | async-done | bytes 589840 | tf_op jit(solution)/shard_map/while
  (223 shorter events, 199.9 us)
Async XLA Ops:
  10.2 202.9 %all-reduce.5.cloned.1.call-start = ((), (), s32[]{:S(2)}) async-start(), calls=%async_computation | async-start | bytes 1179648 | tf_op jit(solution)/shard_map/while
  53.7 5.9 copy-start.3
  214.1 9.7 collective-permute-start
  223.8 195.6 %all-reduce.5.cloned.1.call-start = ((), (), s32[]{:S(2)}) async-start(), calls=%async_computation | async-start | bytes 1179648 | tf_op jit(solution)/shard_map/while
  420.5 9.7 collective-permute-start
  430.2 195.6 %all-reduce.5.cloned.1.call-start = ((), (), s32[]{:S(2)}) async-start(), calls=%async_computation | async-start | bytes 1179648 | tf_op jit(solution)/shard_map/while
  468.3 5.9 copy-start.3
  626.8 9.7 collective-permute-start
  636.6 195.6 %all-reduce.5.cloned.1.call-start = ((), (), s32[]{:S(2)}) async-start(), calls=%async_computation | async-start | bytes 1179648 | tf_op jit(solution)/shard_map/while
  833.2 9.7 collective-permute-start
  843.0 195.6 %all-reduce.5.cloned.1.call-start = ((), (), s32[]{:S(2)}) async-start(), calls=%async_computation | async-start | bytes 1179648 | tf_op jit(solution)/shard_map/while
  1039.6 9.7 collective-permute-start
  1049.3 195.6 %all-reduce.5.cloned.1.call-start = ((), (), s32[]{:S(2)}) async-start(), calls=%async_computation | async-start | bytes 1179648 | tf_op jit(solution)/shard_map/while
  1246.0 9.7 collective-permute-start
  1255.7 195.6 %all-reduce.5.cloned.1.call-start = ((), (), s32[]{:S(2)}) async-start(), calls=%async_computation | async-start | bytes 1179648 | tf_op jit(solution)/shard_map/while
  1452.3 9.7 collective-permute-start
  1462.1 195.6 %all-reduce.5.cloned.1.call-start = ((), (), s32[]{:S(2)}) async-start(), calls=%async_computation | async-start | bytes 1179648 | tf_op jit(solution)/shard_map/while
  1658.7 9.7 collective-permute-start
  1668.5 195.6 %all-reduce.5.cloned.1.call-start = ((), (), s32[]{:S(2)}) async-start(), calls=%async_computation | async-start | bytes 1179648 | tf_op jit(solution)/shard_map/while
  1865.1 9.7 collective-permute-start
  1874.8 195.6 %all-reduce.5.cloned.1.call-start = ((), (), s32[]{:S(2)}) async-start(), calls=%async_computation | async-start | bytes 1179648 | tf_op jit(solution)/shard_map/while
  2071.5 9.7 collective-permute-start
  2081.2 195.6 %all-reduce.5.cloned.1.call-start = ((), (), s32[]{:S(2)}) async-start(), calls=%async_computation | async-start | bytes 1179648 | tf_op jit(solution)/shard_map/while
  2277.8 9.7 collective-permute-start
  (22 other events, 99.2 us)
Sparse Core Ops, SparseCore 0:
  59.7 153.3 all-reduce.4
  267.9 151.5 all-reduce.4
  474.3 151.5 all-reduce.4
  680.6 151.5 all-reduce.4
  887.0 151.5 all-reduce.4
  1093.4 151.5 all-reduce.4
  1299.8 151.5 all-reduce.4
  1506.1 151.5 all-reduce.4
  1712.5 151.5 all-reduce.4
  1918.9 151.5 all-reduce.4
  2125.3 151.5 all-reduce.4
where the time goes:
time: 2300 us; the launch traced here: 2290 us
  waiting for transfers between devices  1680 us (73%)
  blocking collectives  409 us (18%)
  starting transfers between devices  79.4 us (3%)
  matrix products  63.8 us (3%)
  other arithmetic  26.4 us (1%)
    while x22, waiting for transfers between devices  1660 us
    all_gather x11, blocking collectives, advance(): lax.all_gather(upstream.astype(jnp.bfloat16), 'feat', axis=0, tiled=True)  409 us
    ppermute x11, starting transfers between devices, passed_along(): lax.ppermute(value, axis, [(source, source + steps) for source in range(f...  78.9 us
  transfers between devices with their start and end apart: 22, of which 22 were waited for; matrix products, arithmetic and copies ran while one was open for 0% of the time, Pallas kernels for 0%

commit v1 on v0

--- a/solution.py
+++ b/solution.py
@@ -49,7 +49,12 @@
             tile_count * group_rows, feat_dev
         )
         scores = lax.dot_general(
-            lax.all_gather(upstream.astype(jnp.bfloat16), "feat", axis=0, tiled=True),
+            jnp.concatenate(
+                lax.all_to_all(
+                    jnp.stack([upstream.astype(jnp.bfloat16)] * lax.axis_size("feat")), "feat", 0, 0
+                ),
+                axis=0,
+            ),
             dec_rows,
             (((1,), (1,)), ((), ())),
             preferred_element_type=jnp.float32,

time: 2300 us -> 2050 us (0.89)
  blocking collectives: 409 us -> 0 us
  waiting for transfers between devices: 1680 us -> 1760 us
  starting transfers between devices: 79.4 us -> 148 us
    all_gather x11 -> x0, blocking collectives: 409 us -> none  [advance(): lax.all_gather(upstream.astype(jnp.bfloat16), 'feat', axis=0, tiled=True)]
    all_to_all x0 -> x11, waiting for transfers between devices: none -> 200 us  [advance(): lax.all_to_all(jnp.stack([upstream.astype(jnp.bfloat16)] * lax.axis_size(...]
    while x22, waiting for transfers between devices: 1660 us -> 1530 us
    all_to_all x0 -> x11, starting transfers between devices: none -> 68.2 us  [advance(): lax.all_to_all(jnp.stack([upstream.astype(jnp.bfloat16)] * lax.axis_size(...]
  transfers between devices with their start and end apart: 22 -> 33, of which waited for: 22 -> 33; matrix products, arithmetic and copies ran while one was open for 0% -> 1% of each run, Pallas kernels for 0% -> 0%
where the time goes in v1:
time: 2050 us
  waiting for transfers between devices  1760 us (86%)
  starting transfers between devices  148 us (7%)
  matrix products  63.7 us (3%)
  other arithmetic  26.4 us (1%)
  local copies, waits for them, and re-layouts  24.1 us (1%)
    while x22, waiting for transfers between devices  1530 us
    all_to_all x11, waiting for transfers between devices, advance(): lax.all_to_all(jnp.stack([upstream.astype(jnp.bfloat16)] * lax.axis_size(...  200 us
    ppermute x11, starting transfers between devices, passed_along(): lax.ppermute(value, axis, [(source, source + steps) for source in range(f...  78.9 us
    all_to_all x11, starting transfers between devices, advance(): lax.all_to_all(jnp.stack([upstream.astype(jnp.bfloat16)] * lax.axis_size(...  68.2 us
    dot_general x11, matrix products, advance(): lax.dot_general(jnp.concatenate(lax.all_to_all(jnp.stack([upstream.astype...  44.2 us
  transfers between devices with their start and end apart: 33, of which 33 were waited for; matrix products, arithmetic and copies ran while one was open for 1% of the time, Pallas kernels for 0%

profile of v1, /device:TPU:1, one launch (start us, length us, event | category | flops | bytes accessed | tf_op | source)
XLA Modules:
  0.0 2045.4 jit_solution(17402794585922310879)
XLA Ops:
  10.1 2027.9 %while.20 = (s32[]{:T(128)}, f32[2,4608]{1,0:T(2,128)S(1)}, bf16[32,8,512]{2,1,0:T(8,128)(2,1)S(1)}, f32[8,4608]{1,0:T(8,128)S(1)}, pred[]{:T(512)}, /*index=5*/...) while((s32[]{:T(128)}, f32[2,4608]{1,0:T(2,128)S(1)}, ...), condition=%wide.region_3.4_spmd.clone, body=%wide.region_1.3_spmd.clone.sunk | while | flops 604802048 | bytes 38009356 | solution.py:86
  12.2 11.9 all-to-all-start
  24.3 17.4 all-to-all-done
  49.0 141.3 %all-reduce.5.cloned.1.call-done = bf16[64,4608]{1,0:T(8,128)(2,1)} async-done(((bf16[64,4608]{1,0:T(8,128)(2,1)}), bf16[64,4608]{1,0:T(8,128)(2,1)}) %all-reduce.5.cloned.1.call-update) | async-done | bytes 589840 | tf_op jit(solution)/shard_map/while
  209.0 18.3 all-to-all-done
  234.7 139.3 %all-reduce.5.cloned.1.call-done = bf16[64,4608]{1,0:T(8,128)(2,1)} async-done(((bf16[64,4608]{1,0:T(8,128)(2,1)}), bf16[64,4608]{1,0:T(8,128)(2,1)}) %all-reduce.5.cloned.1.call-update) | async-done | bytes 589840 | tf_op jit(solution)/shard_map/while
  392.7 18.3 all-to-all-done
  418.3 139.3 %all-reduce.5.cloned.1.call-done = bf16[64,4608]{1,0:T(8,128)(2,1)} async-done(((bf16[64,4608]{1,0:T(8,128)(2,1)}), bf16[64,4608]{1,0:T(8,128)(2,1)}) %all-reduce.5.cloned.1.call-update) | async-done | bytes 589840 | tf_op jit(solution)/shard_map/while
  576.4 18.3 all-to-all-done
  602.0 139.4 %all-reduce.5.cloned.1.call-done = bf16[64,4608]{1,0:T(8,128)(2,1)} async-done(((bf16[64,4608]{1,0:T(8,128)(2,1)}), bf16[64,4608]{1,0:T(8,128)(2,1)}) %all-reduce.5.cloned.1.call-update) | async-done | bytes 589840 | tf_op jit(solution)/shard_map/while
  760.1 18.3 all-to-all-done
  785.8 139.3 %all-reduce.5.cloned.1.call-done = bf16[64,4608]{1,0:T(8,128)(2,1)} async-done(((bf16[64,4608]{1,0:T(8,128)(2,1)}), bf16[64,4608]{1,0:T(8,128)(2,1)}) %all-reduce.5.cloned.1.call-update) | async-done | bytes 589840 | tf_op jit(solution)/shard_map/while
  943.8 18.3 all-to-all-done
  969.5 139.3 %all-reduce.5.cloned.1.call-done = bf16[64,4608]{1,0:T(8,128)(2,1)} async-done(((bf16[64,4608]{1,0:T(8,128)(2,1)}), bf16[64,4608]{1,0:T(8,128)(2,1)}) %all-reduce.5.cloned.1.call-update) | async-done | bytes 589840 | tf_op jit(solution)/shard_map/while
  1127.5 18.3 all-to-all-done
  1153.2 139.4 %all-reduce.5.cloned.1.call-done = bf16[64,4608]{1,0:T(8,128)(2,1)} async-done(((bf16[64,4608]{1,0:T(8,128)(2,1)}), bf16[64,4608]{1,0:T(8,128)(2,1)}) %all-reduce.5.cloned.1.call-update) | async-done | bytes 589840 | tf_op jit(solution)/shard_map/while
  1311.2 18.3 all-to-all-done
  1336.9 139.3 %all-reduce.5.cloned.1.call-done = bf16[64,4608]{1,0:T(8,128)(2,1)} async-done(((bf16[64,4608]{1,0:T(8,128)(2,1)}), bf16[64,4608]{1,0:T(8,128)(2,1)}) %all-reduce.5.cloned.1.call-update) | async-done | bytes 589840 | tf_op jit(solution)/shard_map/while
  1494.9 18.3 all-to-all-done
  1520.6 139.3 %all-reduce.5.cloned.1.call-done = bf16[64,4608]{1,0:T(8,128)(2,1)} async-done(((bf16[64,4608]{1,0:T(8,128)(2,1)}), bf16[64,4608]{1,0:T(8,128)(2,1)}) %all-reduce.5.cloned.1.call-update) | async-done | bytes 589840 | tf_op jit(solution)/shard_map/while
  1678.6 18.3 all-to-all-done
  1704.3 139.4 %all-reduce.5.cloned.1.call-done = bf16[64,4608]{1,0:T(8,128)(2,1)} async-done(((bf16[64,4608]{1,0:T(8,128)(2,1)}), bf16[64,4608]{1,0:T(8,128)(2,1)}) %all-reduce.5.cloned.1.call-update) | async-done | bytes 589840 | tf_op jit(solution)/shard_map/while
  1862.3 18.3 all-to-all-done
  1888.0 139.3 %all-reduce.5.cloned.1.call-done = bf16[64,4608]{1,0:T(8,128)(2,1)} async-done(((bf16[64,4608]{1,0:T(8,128)(2,1)}), bf16[64,4608]{1,0:T(8,128)(2,1)}) %all-reduce.5.cloned.1.call-update) | async-done | bytes 589840 | tf_op jit(solution)/shard_map/while
  (245 shorter events, 276.2 us)
Async XLA Ops:
  12.2 29.4 %all-to-all-start = ((bf16[32,2,4608]{2,1,0:T(2,128)(2,1)}), bf16[32,2,4608]{2,1,0:T(2,128)(2,1)S(1)}, u32[]{:S(2)}, u32[]{:S(2)}) async-start(bf16[32,2,4608]{2,1,0:T(2,128)(2,1)} %stack.8), calls=%async_computation | async-start | bytes 1179648 | tf_op jit(solution)/shard_map/while/body/eval_jaxpr/all_to_all | solution.py:53
  24.1 166.2 %all-reduce.5.cloned.1.call-start = ((), (), s32[]{:S(2)}) async-start(), calls=%async_computation.1 | async-start | bytes 1179648 | tf_op jit(solution)/shard_map/while
  203.1 24.1 %all-to-all-start = ((bf16[32,2,4608]{2,1,0:T(2,128)(2,1)}), bf16[32,2,4608]{2,1,0:T(2,128)(2,1)S(1)}, u32[]{:S(2)}, u32[]{:S(2)}) async-start(bf16[32,2,4608]{2,1,0:T(2,128)(2,1)} %stack.8), calls=%async_computation | async-start | bytes 1179648 | tf_op jit(solution)/shard_map/while/body/eval_jaxpr/all_to_all | solution.py:53
  208.8 165.2 %all-reduce.5.cloned.1.call-start = ((), (), s32[]{:S(2)}) async-start(), calls=%async_computation.1 | async-start | bytes 1179648 | tf_op jit(solution)/shard_map/while
  386.8 24.1 %all-to-all-start = ((bf16[32,2,4608]{2,1,0:T(2,128)(2,1)}), bf16[32,2,4608]{2,1,0:T(2,128)(2,1)S(1)}, u32[]{:S(2)}, u32[]{:S(2)}) async-start(bf16[32,2,4608]{2,1,0:T(2,128)(2,1)} %stack.8), calls=%async_computation | async-start | bytes 1179648 | tf_op jit(solution)/shard_map/while/body/eval_jaxpr/all_to_all | solution.py:53
  392.4 165.2 %all-reduce.5.cloned.1.call-start = ((), (), s32[]{:S(2)}) async-start(), calls=%async_computation.1 | async-start | bytes 1179648 | tf_op jit(solution)/shard_map/while
  558.7 9.7 collective-permute-start
  570.5 24.1 %all-to-all-start = ((bf16[32,2,4608]{2,1,0:T(2,128)(2,1)}), bf16[32,2,4608]{2,1,0:T(2,128)(2,1)S(1)}, u32[]{:S(2)}, u32[]{:S(2)}) async-start(bf16[32,2,4608]{2,1,0:T(2,128)(2,1)} %stack.8), calls=%async_computation | async-start | bytes 1179648 | tf_op jit(solution)/shard_map/while/body/eval_jaxpr/all_to_all | solution.py:53
  576.1 165.3 %all-reduce.5.cloned.1.call-start = ((), (), s32[]{:S(2)}) async-start(), calls=%async_computation.1 | async-start | bytes 1179648 | tf_op jit(solution)/shard_map/while
  742.4 9.7 collective-permute-start
  754.2 24.1 %all-to-all-start = ((bf16[32,2,4608]{2,1,0:T(2,128)(2,1)}), bf16[32,2,4608]{2,1,0:T(2,128)(2,1)S(1)}, u32[]{:S(2)}, u32[]{:S(2)}) async-start(bf16[32,2,4608]{2,1,0:T(2,128)(2,1)} %stack.8), calls=%async_computation | async-start | bytes 1179648 | tf_op jit(solution)/shard_map/while/body/eval_jaxpr/all_to_all | solution.py:53
  759.9 165.2 %all-reduce.5.cloned.1.call-start = ((), (), s32[]{:S(2)}) async-start(), calls=%async_computation.1 | async-start | bytes 1179648 | tf_op jit(solution)/shard_map/while
  937.9 24.1 %all-to-all-start = ((bf16[32,2,4608]{2,1,0:T(2,128)(2,1)}), bf16[32,2,4608]{2,1,0:T(2,128)(2,1)S(1)}, u32[]{:S(2)}, u32[]{:S(2)}) async-start(bf16[32,2,4608]{2,1,0:T(2,128)(2,1)} %stack.8), calls=%async_computation | async-start | bytes 1179648 | tf_op jit(solution)/shard_map/while/body/eval_jaxpr/all_to_all | solution.py:53
  943.6 165.2 %all-reduce.5.cloned.1.call-start = ((), (), s32[]{:S(2)}) async-start(), calls=%async_computation.1 | async-start | bytes 1179648 | tf_op jit(solution)/shard_map/while
  1121.6 24.1 %all-to-all-start = ((bf16[32,2,4608]{2,1,0:T(2,128)(2,1)}), bf16[32,2,4608]{2,1,0:T(2,128)(2,1)S(1)}, u32[]{:S(2)}, u32[]{:S(2)}) async-start(bf16[32,2,4608]{2,1,0:T(2,128)(2,1)} %stack.8), calls=%async_computation | async-start | bytes 1179648 | tf_op jit(solution)/shard_map/while/body/eval_jaxpr/all_to_all | solution.py:53
  1127.3 165.3 %all-reduce.5.cloned.1.call-start = ((), (), s32[]{:S(2)}) async-start(), calls=%async_computation.1 | async-start | bytes 1179648 | tf_op jit(solution)/shard_map/while
  1305.3 24.1 %all-to-all-start = ((bf16[32,2,4608]{2,1,0:T(2,128)(2,1)}), bf16[32,2,4608]{2,1,0:T(2,128)(2,1)S(1)}, u32[]{:S(2)}, u32[]{:S(2)}) async-start(bf16[32,2,4608]{2,1,0:T(2,128)(2,1)} %stack.8), calls=%async_computation | async-start | bytes 1179648 | tf_op jit(solution)/shard_map/while/body/eval_jaxpr/all_to_all | solution.py:53
  1311.0 165.2 %all-reduce.5.cloned.1.call-start = ((), (), s32[]{:S(2)}) async-start(), calls=%async_computation.1 | async-start | bytes 1179648 | tf_op jit(solution)/shard_map/while
  1489.0 24.1 %all-to-all-start = ((bf16[32,2,4608]{2,1,0:T(2,128)(2,1)}), bf16[32,2,4608]{2,1,0:T(2,128)(2,1)S(1)}, u32[]{:S(2)}, u32[]{:S(2)}) async-start(bf16[32,2,4608]{2,1,0:T(2,128)(2,1)} %stack.8), calls=%async_computation | async-start | bytes 1179648 | tf_op jit(solution)/shard_map/while/body/eval_jaxpr/all_to_all | solution.py:53
  1494.7 165.2 %all-reduce.5.cloned.1.call-start = ((), (), s32[]{:S(2)}) async-start(), calls=%async_computation.1 | async-start | bytes 1179648 | tf_op jit(solution)/shard_map/while
  1672.7 24.1 %all-to-all-start = ((bf16[32,2,4608]{2,1,0:T(2,128)(2,1)}), bf16[32,2,4608]{2,1,0:T(2,128)(2,1)S(1)}, u32[]{:S(2)}, u32[]{:S(2)}) async-start(bf16[32,2,4608]{2,1,0:T(2,128)(2,1)} %stack.8), calls=%async_computation | async-start | bytes 1179648 | tf_op jit(solution)/shard_map/while/body/eval_jaxpr/all_to_all | solution.py:53
  1678.4 165.3 %all-reduce.5.cloned.1.call-start = ((), (), s32[]{:S(2)}) async-start(), calls=%async_computation.1 | async-start | bytes 1179648 | tf_op jit(solution)/shard_map/while
  1856.5 24.1 %all-to-all-start = ((bf16[32,2,4608]{2,1,0:T(2,128)(2,1)}), bf16[32,2,4608]{2,1,0:T(2,128)(2,1)S(1)}, u32[]{:S(2)}, u32[]{:S(2)}) async-start(bf16[32,2,4608]{2,1,0:T(2,128)(2,1)} %stack.8), calls=%async_computation | async-start | bytes 1179648 | tf_op jit(solution)/shard_map/while/body/eval_jaxpr/all_to_all | solution.py:53
  1862.1 165.2 %all-reduce.5.cloned.1.call-start = ((), (), s32[]{:S(2)}) async-start(), calls=%async_computation.1 | async-start | bytes 1179648 | tf_op jit(solution)/shard_map/while
  (33 other events, 197.7 us)
Sparse Core Ops, SparseCore 0:
  47.9 142.3 all-reduce.4
  233.5 140.4 all-reduce.4
  417.2 140.4 all-reduce.4
  600.9 140.5 all-reduce.4
  784.6 140.4 all-reduce.4
  968.3 140.4 all-reduce.4
  1152.0 140.5 all-reduce.4
  1335.7 140.4 all-reduce.4
  1519.4 140.4 all-reduce.4
  1703.1 140.5 all-reduce.4
  1886.8 140.4 all-reduce.4
